TPU v7x, 32 devices: a whole 2x2x4 slice. The times are simulated.
32 devices in a mesh: row: 8 (over z, x), col: 4 (over y, core).
Axes of the slice: x: 2, y: 2, z: 4, core: 2. Of those that a mesh axis runs over, the one named last changes fastest.
Arguments:
- block_input: float32 [4096, 1024], P(('row', 'col')), as said below
- segment_ids: int32 [8, 512], P('row'), may hold values from 0 to 2, never falling along the last dimension, each value on 1 to 384 neighbouring positions
- expert_routes: int32 [4096, 8], P(('row', 'col')), may hold values from 0 to 31, all different within a row; in each aligned block of 128 rows (0 to 127, 128 to 255, ...) at most 36 rows name the same one
- route_weights: float32 [4096, 8], P(('row', 'col')), may hold values from 0.05 to 0.5
- attn_gain: float32 [1024], replicated, may hold values from 0.5 to 1.5
- mlp_gain: float32 [1024], replicated, may hold values from 0.5 to 1.5
- joined_projection_weight: bfloat16 [1024, 2048], P('row', 'col')
- output_weight: bfloat16 [1024, 1024], P('row', 'col'), may hold values from -1 to 1
- w_gate: bfloat16 [32, 1024, 512], P('row', 'col'), may hold values from -0.1875 to 0.1875
- w_up: bfloat16 [32, 1024, 512], P('row', 'col'), may hold values from -0.1875 to 0.1875
- w_down: bfloat16 [32, 512, 1024], P('row', 'col'), may hold values from -0.5 to 0.5
- out_grad: float32 [4096, 1024], P(('row', 'col')), as said below
Outputs:
- block_output: float32 [4096, 1024], P(('row', 'col'))
- input_grad: float32 [4096, 1024], P(('row', 'col'))
- attn_gain_grad: float32 [1024], replicated
- mlp_gain_grad: float32 [1024], replicated
- w_qkv_grad: float32 [1024, 2048], P('row', 'col')
- w_out_grad: float32 [1024, 1024], P('row', 'col')
- w_gate_grad: float32 [32, 1024, 512], P('row', 'col')
- w_up_grad: float32 [32, 1024, 512], P('row', 'col')
- w_down_grad: float32 [32, 512, 1024], P('row', 'col')
Inputs may be any that keep to these rules, and one draw needn't show every extreme that they name: `segment_ids`: each packed row of 512 positions holds whole documents: its ids never fall, each document has 1 to 384 positions, one exactly 384. `expert_routes`: the 8 experts of a token differ. In each aligned block of 128 tokens (the tokens of one device) no expert is named by more than 36 tokens, a bound that some block reaches. `block_input`: feature scales differ from column to column and token scales from row to row. `out_grad`: rows have differing scales.
All inputs are finite; a program needn't handle non-finite values.
Results may differ from a plain program's by a relative error of at most 0.013.
The roundings to bfloat16 on the way count: a program that leaves them out, or rounds other values in their place, can miss the bound.
Values may be sent and summed in bfloat16 or wider, within the bound.
A program may use at most 128 MiB of HBM per device.

v0:
```python
import math

import jax
import jax.numpy as jnp
from jax import lax
from jax.sharding import PartitionSpec as P

HEAD_SIZE = 64
E = 32
PACKED_LENGTH = 512
CAP = 36


EPS = 1e-06


def normalize(values, gains):
    scales = lax.rsqrt(jnp.mean(values * values, axis=-1, keepdims=True) + EPS)
    return (values * scales * gains, scales)


def norm_grad(values, scales, gains, upstream):
    unit_rows = values * scales
    inner_term = upstream * gains
    gain_part = jnp.sum(upstream * unit_rows, axis=0)
    gradient = scales * (
        inner_term - unit_rows * jnp.mean(inner_term * unit_rows, axis=-1, keepdims=True)
    )
    return (gradient, gain_part)


def rotary_tables(segments, width):
    current = segments[:, :, None]
    earlier = segments[:, None, :]
    starts = jnp.sum((earlier < current).astype(jnp.int32), axis=2)
    where_at = jnp.arange(segments.shape[1], dtype=jnp.int32)[None, :] - starts
    half_dim = HEAD_SIZE // 2
    column = jnp.arange(width, dtype=jnp.int32)
    within = column % HEAD_SIZE
    role_index = column // HEAD_SIZE % 4
    frequency = jnp.exp(-math.log(10000.0) * (within % half_dim).astype(jnp.float32) / half_dim)
    angles = where_at.reshape(-1).astype(jnp.float32)[:, None] * frequency[None, :]
    rotary = (role_index < 3)[None, :]
    first = (within < half_dim)[None, :]
    sine_full = jnp.sin(angles)
    cos_table = jnp.where(rotary, jnp.cos(angles), 1.0)
    sin_forward = jnp.where(rotary, jnp.where(first, -sine_full, sine_full), 0.0)
    same_block = column[:, None] // HEAD_SIZE == column[None, :] // HEAD_SIZE
    partner = column[:, None] % HEAD_SIZE == (within[None, :] + half_dim) % HEAD_SIZE
    swap_matrix = (same_block & partner).astype(jnp.float32)
    return (cos_table, sin_forward, swap_matrix)


def turn_rows(values, cos_table, sine_table, swap_matrix):
    swapped = jnp.dot(
        values, swap_matrix, precision=lax.Precision.HIGHEST, preferred_element_type=jnp.float32
    )
    return values * cos_table + swapped * sine_table


def allowed_table(segments):
    same_doc = segments[:, :, None] == segments[:, None, :]
    ordering = jnp.arange(segments.shape[1])
    causal = ordering[None, :] <= ordering[:, None]
    return same_doc & causal[None]


def head_slice(matrix, start, packs_here):
    return matrix[:, start : start + HEAD_SIZE].reshape(packs_here, PACKED_LENGTH, HEAD_SIZE)


def slot_tables(route_block, weight_block):
    flattened = route_block.reshape(-1)
    matches = (flattened[:, None] == jnp.arange(E, dtype=jnp.int32)[None, :]).astype(jnp.int32)
    ranking = jnp.sum((jnp.cumsum(matches, axis=0) - 1) * matches, axis=1)
    slot_of = flattened * CAP + ranking
    lookup = slot_of[None, :] == jnp.arange(E * CAP, dtype=jnp.int32)[:, None]
    filled = jnp.any(lookup, axis=1)
    token_index = jnp.arange(flattened.shape[0], dtype=jnp.int32) // route_block.shape[1]
    owner_tok = jnp.sum(jnp.where(lookup, token_index[None, :], 0), axis=1)
    weight = jnp.sum(jnp.where(lookup, weight_block.reshape(-1)[None, :], 0.0), axis=1)
    return (slot_of.reshape(route_block.shape), filled, owner_tok, weight)


def shards(
    block_input,
    segment_ids,
    expert_routes,
    route_weights,
    attn_gain,
    mlp_gain,
    joined_projection_weight,
    output_weight,
    w_gate,
    w_up,
    w_down,
    out_grad,
):
    scaling = HEAD_SIZE ** (-0.5)
    width = joined_projection_weight.shape[1]
    groups = width // (4 * HEAD_SIZE)
    packs_here = segment_ids.shape[0]
    row_count = packs_here * PACKED_LENGTH
    attention_normed, attn_scale = normalize(block_input, attn_gain)
    attention_normed = attention_normed.astype(jnp.bfloat16)
    normed_rows = lax.all_gather(attention_normed, "col", axis=0, tiled=True)
    qkv_full, out_full = (
        lax.all_gather(joined_projection_weight, "row", axis=0, tiled=True),
        lax.all_gather(output_weight, "row", axis=0, tiled=True),
    )
    projected = jnp.dot(normed_rows, qkv_full, preferred_element_type=jnp.float32)
    cos_table, sin_forward, swap_matrix = rotary_tables(segment_ids, width)
    prepared = turn_rows(projected, cos_table, sin_forward, swap_matrix).astype(jnp.bfloat16)
    allowed = allowed_table(segment_ids)
    head_outputs = []
    log_totals = []
    for group in range(groups):
        base = group * 4 * HEAD_SIZE
        key_block = head_slice(prepared, base + 2 * HEAD_SIZE, packs_here)
        value_block = head_slice(prepared, base + 3 * HEAD_SIZE, packs_here)
        for inner in range(2):
            query_block = head_slice(prepared, base + inner * HEAD_SIZE, packs_here)
            scored = (
                jnp.einsum(
                    "pqd,pkd->pqk", query_block, key_block, preferred_element_type=jnp.float32
                )
                * scaling
            )
            scored = jnp.where(allowed, scored, -1e30)
            row_max = jnp.max(scored, axis=-1)
            log_total = row_max + jnp.log(jnp.sum(jnp.exp(scored - row_max[..., None]), axis=-1))
            probability = jnp.where(allowed, jnp.exp(scored - log_total[..., None]), 0.0).astype(
                jnp.bfloat16
            )
            result = jnp.einsum(
                "pqk,pkd->pqd", probability, value_block, preferred_element_type=jnp.float32
            ).astype(jnp.bfloat16)
            head_outputs.append(result.reshape(row_count, HEAD_SIZE))
            log_totals.append(log_total)
    heads_flat = jnp.concatenate(head_outputs, axis=1)
    row_block = heads_flat
    attention = lax.psum_scatter(
        jnp.einsum("tj,dj->td", row_block, out_full, preferred_element_type=jnp.float32),
        "col",
        scatter_dimension=0,
        tiled=True,
    )
    residual = block_input + attention
    mlp_normed, mlp_scale = normalize(residual, mlp_gain)
    mlp_normed = mlp_normed.astype(jnp.bfloat16)
    slot_of, filled, owner_tok, weight = slot_tables(expert_routes, route_weights)
    outgoing = jnp.where(filled[:, None], mlp_normed[owner_tok], 0).reshape(E, CAP, -1)
    gate_full, up_full, down_full = (
        lax.all_gather(w_gate, "col", axis=1, tiled=True),
        lax.all_gather(w_up, "col", axis=1, tiled=True),
        lax.all_gather(w_down, "col", axis=1, tiled=True),
    )
    arrived = lax.all_to_all(outgoing, "row", split_axis=0, concat_axis=1, tiled=True)
    gate_pre = jnp.einsum("erd,edf->erf", arrived, gate_full, preferred_element_type=jnp.float32)
    up_pre = jnp.einsum("erd,edf->erf", arrived, up_full, preferred_element_type=jnp.float32)
    sigmoid_gate = jax.nn.sigmoid(gate_pre)
    active = (gate_pre * sigmoid_gate * up_pre).astype(jnp.bfloat16)
    produced = jnp.einsum(
        "erf,efd->erd", active, down_full, preferred_element_type=jnp.float32
    ).astype(jnp.bfloat16)
    returned = lax.all_to_all(produced, "row", split_axis=1, concat_axis=0, tiled=True).reshape(
        E * CAP, -1
    )
    picked = returned[slot_of].astype(jnp.float32)
    block_output = residual + jnp.sum(route_weights[..., None] * picked, axis=1)
    cot_slots = (
        jnp.where(filled[:, None], weight[:, None] * out_grad[owner_tok], 0.0)
        .astype(jnp.bfloat16)
        .reshape(E, CAP, -1)
    )
    cot_arrived = lax.all_to_all(cot_slots, "row", split_axis=0, concat_axis=1, tiled=True)
    gate_back, up_back, down_back = (gate_full, up_full, down_full)
    act_grad = jnp.einsum(
        "erd,efd->erf", cot_arrived, down_back, preferred_element_type=jnp.float32
    )
    down_grad = jnp.einsum("erf,erd->efd", active, cot_arrived, preferred_element_type=jnp.float32)
    gate_grad = (act_grad * up_pre * sigmoid_gate * (1.0 + gate_pre * (1.0 - sigmoid_gate))).astype(
        jnp.bfloat16
    )
    up_grad = (act_grad * gate_pre * sigmoid_gate).astype(jnp.bfloat16)
    gate_w_grad = jnp.einsum("erd,erf->edf", arrived, gate_grad, preferred_element_type=jnp.float32)
    up_w_grad = jnp.einsum("erd,erf->edf", arrived, up_grad, preferred_element_type=jnp.float32)
    row_grad = jnp.einsum("erf,edf->erd", gate_grad, gate_back, preferred_element_type=jnp.float32)
    row_grad = (
        row_grad + jnp.einsum("erf,edf->erd", up_grad, up_back, preferred_element_type=jnp.float32)
    ).astype(jnp.bfloat16)
    grad_back = lax.all_to_all(row_grad, "row", split_axis=1, concat_axis=0, tiled=True).reshape(
        E * CAP, -1
    )
    mlp_normed_grad = jnp.sum(grad_back[slot_of].astype(jnp.float32), axis=1)
    gate_share, up_share, down_share = (
        lax.psum_scatter(gate_w_grad, "col", scatter_dimension=1, tiled=True),
        lax.psum_scatter(up_w_grad, "col", scatter_dimension=1, tiled=True),
        lax.psum_scatter(down_grad, "col", scatter_dimension=1, tiled=True),
    )
    residual_part, mlp_part = norm_grad(residual, mlp_scale, mlp_gain, mlp_normed_grad)
    residual_grad = out_grad + residual_part
    residual_cotangent = residual_grad.astype(jnp.bfloat16)
    cot_rows = lax.all_gather(residual_cotangent, "col", axis=0, tiled=True)
    heads_cotangent = jnp.einsum(
        "td,dj->tj", cot_rows, out_full, preferred_element_type=jnp.float32
    ).astype(jnp.bfloat16)
    out_grad_part = jnp.einsum(
        "td,tj->dj", cot_rows, heads_flat, preferred_element_type=jnp.float32
    )
    grad_pieces = []
    for group in range(groups):
        base = group * 4 * HEAD_SIZE
        key_block = head_slice(prepared, base + 2 * HEAD_SIZE, packs_here)
        value_block = head_slice(prepared, base + 3 * HEAD_SIZE, packs_here)
        key_gradient = jnp.zeros((packs_here, PACKED_LENGTH, HEAD_SIZE), jnp.float32)
        value_gradient = jnp.zeros((packs_here, PACKED_LENGTH, HEAD_SIZE), jnp.float32)
        query_parts = []
        for inner in range(2):
            head_number = 2 * group + inner
            query_block = head_slice(prepared, base + inner * HEAD_SIZE, packs_here)
            cot_block = head_slice(heads_cotangent, head_number * HEAD_SIZE, packs_here)
            result_block = head_slice(heads_flat, head_number * HEAD_SIZE, packs_here)
            scored = (
                jnp.einsum(
                    "pqd,pkd->pqk", query_block, key_block, preferred_element_type=jnp.float32
                )
                * scaling
            )
            scored = jnp.where(allowed, scored, -1e30)
            probability = jnp.where(
                allowed, jnp.exp(scored - log_totals[head_number][..., None]), 0.0
            )
            value_gradient = value_gradient + jnp.einsum(
                "pqk,pqd->pkd",
                probability.astype(jnp.bfloat16),
                cot_block,
                preferred_element_type=jnp.float32,
            )
            prob_grad = jnp.einsum(
                "pqd,pkd->pqk", cot_block, value_block, preferred_element_type=jnp.float32
            )
            row_delta = jnp.einsum(
                "pqd,pqd->pq", cot_block, result_block, preferred_element_type=jnp.float32
            )
            score_grad = (probability * (prob_grad - row_delta[..., None]) * scaling).astype(
                jnp.bfloat16
            )
            query_parts.append(
                jnp.einsum(
                    "pqk,pkd->pqd", score_grad, key_block, preferred_element_type=jnp.float32
                ).reshape(row_count, HEAD_SIZE)
            )
            key_gradient = key_gradient + jnp.einsum(
                "pqk,pqd->pkd", score_grad, query_block, preferred_element_type=jnp.float32
            )
        grad_pieces.extend(query_parts)
        grad_pieces.append(key_gradient.reshape(row_count, HEAD_SIZE))
        grad_pieces.append(value_gradient.reshape(row_count, HEAD_SIZE))
    raw_grad = jnp.concatenate(grad_pieces, axis=1)
    projected_grad = turn_rows(raw_grad, cos_table, -sin_forward, swap_matrix).astype(jnp.bfloat16)
    qkv_grad_part = jnp.einsum(
        "td,tj->dj", normed_rows, projected_grad, preferred_element_type=jnp.float32
    )
    qkv_share, out_share = (
        lax.psum_scatter(qkv_grad_part, "row", scatter_dimension=0, tiled=True),
        lax.psum_scatter(out_grad_part, "row", scatter_dimension=0, tiled=True),
    )
    row_block = projected_grad
    attn_normed_grad = lax.psum_scatter(
        jnp.einsum("tj,dj->td", row_block, qkv_full, preferred_element_type=jnp.float32),
        "col",
        scatter_dimension=0,
        tiled=True,
    )
    input_part, attn_part = norm_grad(block_input, attn_scale, attn_gain, attn_normed_grad)
    input_grad = residual_grad + input_part
    attn_gain_grad, mlp_gain_grad = lax.psum((attn_part, mlp_part), ("row", "col"))
    return (
        block_output,
        input_grad,
        attn_gain_grad,
        mlp_gain_grad,
        qkv_share,
        out_share,
        gate_share,
        up_share,
        down_share,
    )


def solution(mesh):
    in_specs = (
        P(("row", "col"), None),
        P("row", None),
        P(("row", "col"), None),
        P(("row", "col"), None),
        P(),
        P(),
        P("row", "col"),
        P("row", "col"),
        P("row", "col", None),
        P("row", "col", None),
        P("row", "col", None),
        P(("row", "col"), None),
    )
    out_specs = (
        P(("row", "col"), None),
        P(("row", "col"), None),
        P(),
        P(),
        P("row", "col"),
        P("row", "col"),
        P("row", "col", None),
        P("row", "col", None),
        P("row", "col", None),
    )
    return jax.shard_map(shards, mesh=mesh, in_specs=in_specs, out_specs=out_specs, check_vma=False)
```

profile of v0, /device:TPU:0, one launch (start us, length us, event | category | flops | bytes accessed | tf_op | source)
XLA Modules:
  0.0 844.1 jit_solution(800376743280248962)
XLA Ops:
  12.2 33.6 %all_gather.23 = bf16[1024,256]{1,0:T(8,128)(2,1)S(1)} all-gather(bf16[128,256]{1,0:T(8,128)(2,1)} %param.19), channel_id=1, replica_groups=mesh['row'=8,'col'=4] {'row'}, dimensions={0}, use_global_device_ids=true | all-gather | bytes 589824 | tf_op jit(solution)/shard_map/all_gather | solution.py:109
  45.8 26.5 %all-gather.9.cloned.1.call-done = bf16[1024,512]{1,0:T(8,128)(2,1)} async-done(((bf16[128,512]{1,0:T(8,128)(2,1)}), bf16[1024,512]{1,0:T(8,128)(2,1)}) %all-gather.9.cloned.1.call-update) | async-done | bytes 1048592 | tf_op jit(solution)/shard_map/all_gather | solution.py:108
  74.6 5.3 fusion.28
  88.1 9.0 %reduce-window.6 = s32[32,8,128]{2,1,0:T(8,128)S(1)} reduce-window(s32[32,8,128]{2,1,0:T(8,128)S(1)} %fusion.62, s32[]{:T(128)} %constant.133.clone.1), window={size=1x1x128 pad=0_0x0_0x127_0}, to_apply=%region_11.12 | reduce-window | flops 4161536 | bytes 262148 | tf_op jit(solution)/shard_map/reduce-window
  134.2 42.7 %all-to-all-done.2 = bf16[32,36,1024]{2,1,0:T(8,128)(2,1)} async-done(((bf16[32,36,1024]{2,1,0:T(8,128)(2,1)}), bf16[32,36,1024]{2,1,0:T(8,128)(2,1)}, u32[]{:S(2)}, u32[]{:S(2)}) %all-to-all-start.2) | async-done | bytes 2359328 | tf_op jit(solution)/shard_map/all_to_all | solution.py:176
  186.3 54.0 %all-to-all-done = bf16[32,36,1024]{2,1,0:T(8,128)(2,1)} async-done(((bf16[32,36,1024]{2,1,0:T(8,128)(2,1)}), bf16[32,36,1024]{2,1,0:T(8,128)(2,1)}, u32[]{:S(2)}, u32[]{:S(2)}) %all-to-all-start) | async-done | bytes 2359328 | tf_op jit(solution)/shard_map/all_to_all | solution.py:158
  243.9 6.1 fusion.10
  250.0 5.3 fusion.12
  255.3 7.4 multiply_convert_fusion
  266.2 10.4 %add_convert_fusion = bf16[4,288,1024]{2,1,0:T(8,128)(2,1)S(1)} fusion(f32[4,288,1024]{2,1,0:T(8,128)S(1)} %fusion.135, bf16[4,288,512]{2,1,0:T(8,128)(2,1)S(1)} %get-tuple-element.23, bf16[4,1024,512]{2,1,0:T(8,128)(2,1)S(1)} %copy-done.15), kind=kOutput, calls=%fused_computation.5 | convolution fusion | flops 1210318848 | bytes 12451840 | tf_op jit(solution)/shard_map/erf,edf->erd/dot_general | solution.py:190
  291.0 46.6 %all-to-all-done.3 = bf16[4,288,1024]{2,0,1:T(4,128)(2,1)} async-done(((bf16[4,288,1024]{2,0,1:T(4,128)(2,1)}), bf16[4,288,1024]{2,0,1:T(4,128)(2,1)}, u32[]{:S(2)}, u32[]{:S(2)}) %all-to-all-start.3) | async-done | bytes 2359328 | tf_op jit(solution)/shard_map/all_to_all | solution.py:192
  349.1 5.3 gather_fusion.3
  358.9 36.5 %all-to-all-done.1 = bf16[4,288,1024]{2,0,1:T(4,128)(2,1)} async-done(((bf16[4,288,1024]{2,0,1:T(4,128)(2,1)}), bf16[4,288,1024]{2,0,1:T(4,128)(2,1)}, u32[]{:S(2)}, u32[]{:S(2)}) %all-to-all-start.1) | async-done | bytes 2359328 | tf_op jit(solution)/shard_map/all_to_all | solution.py:166
  402.0 5.3 gather_fusion.1
  412.1 15.7 %all-gather.17.cloned.1.call-done = bf16[512,1024]{1,0:T(8,128)(2,1)} async-done(((bf16[128,1024]{1,0:T(8,128)(2,1)}), bf16[512,1024]{1,0:T(8,128)(2,1)}) %all-gather.17.cloned.1.call-update) | async-done | bytes 1048592 | tf_op jit(solution)/shard_map/all_gather | solution.py:204
  448.8 7.6 fusion.8
  456.4 7.5 fusion.6
  465.6 7.3 fusion.2
  476.0 39.5 %all-reduce = (f32[1024]{0:T(1024)}, f32[1024]{0:T(1024)}) all-reduce(f32[1024]{0:T(1024)S(1)} %get-tuple-element.11, f32[1024]{0:T(1024)S(1)} %get-tuple-element.9), channel_id=1, replica_groups=mesh['row'=8,'col'=4] {'row','col'}, use_global_device_ids=true, to_apply=%region_24.25 | all-reduce | flops 2048 | bytes 16384 | tf_op jit(solution)/shard_map/psum | solution.py:278
  517.6 25.5 %reduce-scatter.14.cloned.1.call-done = f32[128,256]{1,0:T(8,128)} async-done(((f32[1024,256]{1,0:T(8,128)}), f32[128,256]{1,0:T(8,128)}) %reduce-scatter.14.cloned.1.call-update) | async-done | bytes 131088 | tf_op jit(solution)/shard_map/reduce_scatter | solution.py:267
  543.0 71.5 %reduce-scatter.12.cloned.1.call-done = f32[128,512]{1,0:T(8,128)} async-done(((f32[1024,512]{1,0:T(8,128)}), f32[128,512]{1,0:T(8,128)}) %reduce-scatter.12.cloned.1.call-update) | async-done | bytes 262160 | tf_op jit(solution)/shard_map/reduce_scatter | solution.py:266
  614.5 73.6 %reduce-scatter.16.cloned.1.call-done = f32[4,256,512]{2,1,0:T(8,128)} async-done(((f32[4,1024,512]{2,1,0:T(8,128)}), f32[4,256,512]{2,1,0:T(8,128)}) %reduce-scatter.16.cloned.1.call-update) | async-done | bytes 2097168 | tf_op jit(solution)/shard_map/reduce_scatter | solution.py:197
  688.1 74.4 %reduce-scatter.18.cloned.1.call-done = f32[4,256,512]{2,1,0:T(8,128)} async-done(((f32[4,1024,512]{2,1,0:T(8,128)}), f32[4,256,512]{2,1,0:T(8,128)}) %reduce-scatter.18.cloned.1.call-update) | async-done | bytes 2097168 | tf_op jit(solution)/shard_map/reduce_scatter | solution.py:198
  762.5 74.6 %reduce-scatter.20.cloned.1.call-done = f32[4,128,1024]{2,1,0:T(8,128)} async-done(((f32[4,512,1024]{2,1,0:T(8,128)}), f32[4,128,1024]{2,1,0:T(8,128)}) %reduce-scatter.20.cloned.1.call-update) | async-done | bytes 2097168 | tf_op jit(solution)/shard_map/reduce_scatter | solution.py:199
  (274 shorter events, 137.4 us)
Async XLA Ops:
  7.2 38.6 %all-gather.7.cloned.1.call-start = ((), (), s32[]{:S(2)}) async-start(), calls=%async_computation.11 | async-start | bytes 1310720 | tf_op jit(solution)/shard_map/all_gather | solution.py:106
  10.3 62.0 %all-gather.9.cloned.1.call-start = ((), (), s32[]{:S(2)}) async-start(), calls=%async_computation.12 | async-start | bytes 1179648 | tf_op jit(solution)/shard_map/all_gather | solution.py:108
  11.0 108.3 %reduce-scatter.8.cloned.1.call-start = ((), (), s32[]{:S(2)}) async-start(), calls=%async_computation.13 | async-start | bytes 2621440 | tf_op jit(solution)/shard_map/reduce_scatter | solution.py:142
  11.1 68.8 %copy-start.64 = (pred[512]{0:T(512)(128)(4,1)}, pred[512]{0:T(512)(128)(4,1)S(1)}, u32[]{:S(2)}) copy-start(pred[512]{0:T(512)(128)(4,1)S(1)} %get-tuple-element.39) | copy-start | bytes 1540
  11.1 68.8 %copy-start.66 = (pred[512]{0:T(512)(128)(4,1)}, pred[512]{0:T(512)(128)(4,1)S(1)}, u32[]{:S(2)}) copy-start(pred[512]{0:T(512)(128)(4,1)S(1)} %get-tuple-element.40) | copy-start | bytes 1540
  11.1 68.8 %copy-start.57 = (f32[512]{0:T(512)}, f32[512]{0:T(512)S(1)}, u32[]{:S(2)}) copy-start(f32[512]{0:T(512)S(1)} %fusion.114) | copy-start | bytes 6148
  11.2 68.8 %copy-start.59 = (s32[512]{0:T(512)}, s32[512]{0:T(512)S(1)}, u32[]{:S(2)}) copy-start(s32[512]{0:T(512)S(1)} %get-tuple-element.35) | copy-start | bytes 6148
  11.2 68.8 %copy-start.61 = (s32[512]{0:T(512)}, s32[512]{0:T(512)S(1)}, u32[]{:S(2)}) copy-start(s32[512]{0:T(512)S(1)} %get-tuple-element.36) | copy-start | bytes 6148
  12.2 67.8 %copy-start.45 = (s32[512]{0:T(512)}, s32[512]{0:T(512)S(1)}, u32[]{:S(2)}) copy-start(s32[512]{0:T(512)S(1)} %get-tuple-element.37) | copy-start | bytes 6148
  12.2 67.8 %copy-start.47 = (f32[512]{0:T(512)}, f32[512]{0:T(512)S(1)}, u32[]{:S(2)}) copy-start(f32[512]{0:T(512)S(1)} %get-tuple-element.38) | copy-start | bytes 6148
  86.6 157.3 %all-gather.13.cloned.1.call-start = ((), (), s32[]{:S(2)}) async-start(), calls=%async_computation.15 | async-start | bytes 5242880 | tf_op jit(solution)/shard_map/all_gather | solution.py:155
  87.2 162.9 %all-gather.11.cloned.1.call-start = ((), (), s32[]{:S(2)}) async-start(), calls=%async_computation.14 | async-start | bytes 5242880 | tf_op jit(solution)/shard_map/all_gather | solution.py:154
  114.2 62.7 %all-to-all-start.2 = ((bf16[32,36,1024]{2,1,0:T(8,128)(2,1)}), bf16[32,36,1024]{2,1,0:T(8,128)(2,1)}, u32[]{:S(2)}, u32[]{:S(2)}) async-start(bf16[32,36,1024]{2,1,0:T(8,128)(2,1)} %select_convert_fusion), calls=%async_computation.3 | async-start | bytes 5242880 | tf_op jit(solution)/shard_map/all_to_all | solution.py:176
  118.7 136.6 %all-gather.15.cloned.1.call-start = ((), (), s32[]{:S(2)}) async-start(), calls=%async_computation.16 | async-start | bytes 5242880 | tf_op jit(solution)/shard_map/all_gather | solution.py:156
  176.9 63.4 %all-to-all-start = ((bf16[32,36,1024]{2,1,0:T(8,128)(2,1)}), bf16[32,36,1024]{2,1,0:T(8,128)(2,1)}, u32[]{:S(2)}, u32[]{:S(2)}) async-start(bf16[32,36,1024]{2,1,0:T(8,128)(2,1)} %broadcast_select_fusion), calls=%async_computation.1 | async-start | bytes 5242880 | tf_op jit(solution)/shard_map/all_to_all | solution.py:158
  279.8 57.8 %all-to-all-start.3 = ((bf16[4,288,1024]{2,0,1:T(4,128)(2,1)}), bf16[4,288,1024]{2,0,1:T(4,128)(2,1)}, u32[]{:S(2)}, u32[]{:S(2)}) async-start(bf16[4,288,1024]{2,0,1:T(4,128)(2,1)} %copy.127), calls=%async_computation.4 | async-start | bytes 4718592 | tf_op jit(solution)/shard_map/all_to_all | solution.py:192
  337.5 57.8 %all-to-all-start.1 = ((bf16[4,288,1024]{2,0,1:T(4,128)(2,1)}), bf16[4,288,1024]{2,0,1:T(4,128)(2,1)}, u32[]{:S(2)}, u32[]{:S(2)}) async-start(bf16[4,288,1024]{2,0,1:T(4,128)(2,1)} %copy.119), calls=%async_computation.2 | async-start | bytes 4718592 | tf_op jit(solution)/shard_map/all_to_all | solution.py:166
  341.9 85.9 %all-gather.17.cloned.1.call-start = ((), (), s32[]{:S(2)}) async-start(), calls=%async_computation.17 | async-start | bytes 1310720 | tf_op jit(solution)/shard_map/all_gather | solution.py:204
  411.8 62.9 %reduce-scatter.10.cloned.1.call-start = ((), (), s32[]{:S(2)}) async-start(), calls=%async_computation.18 | async-start | bytes 2621440 | tf_op jit(solution)/shard_map/reduce_scatter | solution.py:270
  443.4 99.7 %reduce-scatter.14.cloned.1.call-start = ((), (), s32[]{:S(2)}) async-start(), calls=%async_computation.20 | async-start | bytes 1179648 | tf_op jit(solution)/shard_map/reduce_scatter | solution.py:267
  444.9 169.6 %reduce-scatter.12.cloned.1.call-start = ((), (), s32[]{:S(2)}) async-start(), calls=%async_computation.19 | async-start | bytes 2359296 | tf_op jit(solution)/shard_map/reduce_scatter | solution.py:266
  448.5 239.6 %reduce-scatter.16.cloned.1.call-start = ((), (), s32[]{:S(2)}) async-start(), calls=%async_computation.21 | async-start | bytes 10485760 | tf_op jit(solution)/shard_map/reduce_scatter | solution.py:197
  456.4 306.2 %reduce-scatter.18.cloned.1.call-start = ((), (), s32[]{:S(2)}) async-start(), calls=%async_computation.22 | async-start | bytes 10485760 | tf_op jit(solution)/shard_map/reduce_scatter | solution.py:198
  464.0 373.2 %reduce-scatter.20.cloned.1.call-start = ((), (), s32[]{:S(2)}) async-start(), calls=%async_computation.23 | async-start | bytes 10485760 | tf_op jit(solution)/shard_map/reduce_scatter | solution.py:199
  (61 other events, 340.0 us)
Sparse Core Ops, SparseCore 0:
  10.4 19.4 all-gather.6
  32.0 40.2 all-gather.8
  86.7 29.9 reduce-scatter.7
  118.1 34.4 all-gather.12
  154.1 34.4 all-gather.10
  190.0 34.4 all-gather.14
  411.9 15.8 all-gather.16
  443.5 31.1 reduce-scatter.9
  478.7 64.2 reduce-scatter.13
  547.0 67.4 reduce-scatter.11
  617.7 70.3 reduce-scatter.15
  691.1 71.3 reduce-scatter.17
  765.7 71.3 reduce-scatter.19
where the time goes:
time: 853 us; the launch traced here: 844 us
  waiting for transfers between devices  545 us (64%)
  matrix products  88.1 us (10%)
  blocking collectives  73.1 us (9%)
  local copies, waits for them, and re-layouts  66.8 us (8%)
  other arithmetic  36.2 us (4%)
  starting transfers between devices  18.9 us (2%)
  between operations  15.5 us (2%)
    reduce_scatter x1, waiting for transfers between devices, shards(): lax.psum_scatter(down_grad, 'col', scatter_dimension=1, tiled=True)  74.6 us
    reduce_scatter x1, waiting for transfers between devices, shards(): lax.psum_scatter(up_w_grad, 'col', scatter_dimension=1, tiled=True)  74.4 us
    reduce_scatter x1, waiting for transfers between devices, shards(): lax.psum_scatter(gate_w_grad, 'col', scatter_dimension=1, tiled=True)  73.6 us
    reduce_scatter x1, waiting for transfers between devices, shards(): lax.psum_scatter(qkv_grad_part, 'row', scatter_dimension=0, tiled=True)  71.5 us
    all_to_all x1, waiting for transfers between devices, shards(): lax.all_to_all(outgoing, 'row', split_axis=0, concat_axis=1, tiled=True)  54 us
    all_to_all x1, waiting for transfers between devices, shards(): lax.all_to_all(row_grad, 'row', split_axis=1, concat_axis=0, tiled=True)  46.6 us
    all_to_all x1, waiting for transfers between devices, shards(): lax.all_to_all(cot_slots, 'row', split_axis=0, concat_axis=1, tiled=True)  42.7 us
    psum x1, blocking collectives, shards(): lax.psum((attn_part, mlp_part), ('row', 'col'))  39.5 us
  transfers between devices with their start and end apart: 17, of which 12 were waited for; matrix products, arithmetic and copies ran while one was open for 14% of the time, Pallas kernels for 0%

commit v1 on v0

--- a/solution.py
+++ b/solution.py
@@ -69,17 +69,138 @@
     return matrix[:, start : start + HEAD_SIZE].reshape(packs_here, PACKED_LENGTH, HEAD_SIZE)
 
 
-def slot_tables(route_block, weight_block):
-    flattened = route_block.reshape(-1)
-    matches = (flattened[:, None] == jnp.arange(E, dtype=jnp.int32)[None, :]).astype(jnp.int32)
-    ranking = jnp.sum((jnp.cumsum(matches, axis=0) - 1) * matches, axis=1)
-    slot_of = flattened * CAP + ranking
-    lookup = slot_of[None, :] == jnp.arange(E * CAP, dtype=jnp.int32)[:, None]
-    filled = jnp.any(lookup, axis=1)
-    token_index = jnp.arange(flattened.shape[0], dtype=jnp.int32) // route_block.shape[1]
-    owner_tok = jnp.sum(jnp.where(lookup, token_index[None, :], 0), axis=1)
-    weight = jnp.sum(jnp.where(lookup, weight_block.reshape(-1)[None, :], 0.0), axis=1)
-    return (slot_of.reshape(route_block.shape), filled, owner_tok, weight)
+def col_place():
+    size = lax.axis_size("col")
+    me = lax.axis_index("col")
+    return size // 2, me // 2, me % 2
+
+
+def col_shift(values, shift):
+    size = lax.axis_size("col")
+    pairs = [(i, (i // 2 - shift) % (size // 2) * 2 + i % 2) for i in range(size)]
+    return lax.ppermute(values, "col", pairs)
+
+
+def core_swap(values):
+    size = lax.axis_size("col")
+    return lax.ppermute(values, "col", [(i, i ^ 1) for i in range(size)])
+
+
+def gather_parts(values):
+    chips, _, _ = col_place()
+    same = [values] + [col_shift(values, s) for s in range(1, chips)]
+    return same + [core_swap(part) for part in same]
+
+
+def part_owner(k):
+    chips, chip, core = col_place()
+    side = core if k < chips else 1 - core
+    return (chip + k % chips) % chips * 2 + side
+
+
+def gather_natural(values, axis):
+    parts = gather_parts(values)
+    size = values.shape[axis]
+    shape = list(values.shape)
+    shape[axis] = size * len(parts)
+    whole = jnp.zeros(shape, values.dtype)
+    for k, part in enumerate(parts):
+        whole = lax.dynamic_update_slice_in_dim(whole, part, part_owner(k) * size, axis)
+    return whole
+
+
+def to_relative(values, axis):
+    count = lax.axis_size("col")
+    size = values.shape[axis] // count
+    return jnp.concatenate(
+        [
+            lax.dynamic_slice_in_dim(values, part_owner(k) * size, size, axis)
+            for k in range(count)
+        ],
+        axis=axis,
+    )
+
+
+def to_natural(values, axis):
+    chips, chip, core = col_place()
+    count = lax.axis_size("col")
+    size = values.shape[axis] // count
+    pieces = []
+    for n in range(count):
+        k = (n // 2 - chip) % chips + jnp.where(core == n % 2, 0, chips)
+        pieces.append(lax.dynamic_slice_in_dim(values, k * size, size, axis))
+    return jnp.concatenate(pieces, axis=axis)
+
+
+def scatter_relative(values, axis):
+    chips, _, _ = col_place()
+    half = values.shape[axis] // 2
+    size = half // chips
+    other = lax.slice_in_dim(values, half, 2 * half, axis=axis).astype(jnp.bfloat16)
+    arrived = core_swap(other)
+
+    def part(k):
+        mine = lax.slice_in_dim(values, k * size, (k + 1) * size, axis=axis)
+        got = lax.slice_in_dim(arrived, k * size, (k + 1) * size, axis=axis)
+        return mine.astype(jnp.float32) + got.astype(jnp.float32)
+
+    total = part(0)
+    for s in range(1, chips):
+        total = total + col_shift(part(s).astype(jnp.bfloat16), chips - s).astype(jnp.float32)
+    return total
+
+
+def scatter_natural(values, axis, near=jnp.bfloat16):
+    chips, chip, core = col_place()
+    size = values.shape[axis] // (2 * chips)
+    split = values.shape[:axis] + (chips, 2, size) + values.shape[axis + 1 :]
+    split = values.reshape(split)
+    other = lax.dynamic_index_in_dim(split, 1 - core, axis + 1, keepdims=False)
+    mine = lax.dynamic_index_in_dim(split, core, axis + 1, keepdims=False)
+    arrived = core_swap(other.astype(near))
+
+    def part(s):
+        at = (chip + s) % chips
+        own = lax.dynamic_index_in_dim(mine, at, axis, keepdims=False)
+        got = lax.dynamic_index_in_dim(arrived, at, axis, keepdims=False)
+        return own.astype(jnp.float32) + got.astype(jnp.float32)
+
+    total = part(0)
+    for s in range(1, chips):
+        total = total + col_shift(part(s).astype(jnp.bfloat16), chips - s).astype(jnp.float32)
+    return total
+
+
+def sum_everywhere(values):
+    for name in ("col", "row"):
+        size = lax.axis_size(name)
+        step = 1
+        while step < size:
+            values = values + lax.ppermute(values, name, [(i, i ^ step) for i in range(size)])
+            step *= 2
+    return values
+
+
+def slot_tables(routes, weights, experts, block):
+    first = lax.axis_index("row") * experts
+    wanted = (first + jnp.arange(experts, dtype=jnp.int32)).astype(jnp.float32)
+    match = routes[:, :, None] == wanted[None, None, :]
+    member = jnp.any(match, axis=1)
+    weight = jnp.sum(jnp.where(match, weights[:, :, None], 0.0), axis=1)
+    blocks = routes.shape[0] // block
+    flags = member.astype(jnp.float32).reshape(blocks, block, experts)
+    order = jnp.arange(block)
+    earlier = (order[None, :] < order[:, None]).astype(jnp.float32)
+    inside = jnp.einsum("ij,bje->bie", earlier, flags, preferred_element_type=jnp.float32)
+    order = jnp.arange(blocks)
+    before = (order[None, :] < order[:, None]).astype(jnp.float32)
+    base = jnp.sum(before[:, :, None] * jnp.sum(flags, axis=1)[None], axis=1)
+    rank = (inside + base[:, None, :]).reshape(-1, experts).astype(jnp.int32)
+    slot = jnp.where(member, rank, -1).T
+    slots = jnp.arange(blocks * CAP, dtype=jnp.int32)
+    chosen = slot[:, None, :] == slots[None, :, None]
+    slot_weight = jnp.sum(jnp.where(chosen, weight.T[:, None, :], 0.0), axis=2)
+    return chosen.astype(jnp.bfloat16), slot_weight
 
 
 def shards(
@@ -103,7 +224,26 @@
     row_count = packs_here * PACKED_LENGTH
     attention_normed, attn_scale = normalize(block_input, attn_gain)
     attention_normed = attention_normed.astype(jnp.bfloat16)
-    normed_rows = lax.all_gather(attention_normed, "col", axis=0, tiled=True)
+    normed_rows = gather_natural(attention_normed, 0)
+    route_rows = lax.all_gather(
+        jnp.concatenate([expert_routes.astype(jnp.float32), route_weights], axis=1),
+        "row",
+        axis=0,
+        tiled=True,
+    )
+    picks = expert_routes.shape[1]
+    experts = w_gate.shape[0]
+    chosen, slot_weight = slot_tables(
+        route_rows[:, :picks], route_rows[:, picks:], experts, block_input.shape[0]
+    )
+    pick_matrix = chosen.reshape(-1, chosen.shape[2])
+    cot_rows_in = lax.all_gather(out_grad.astype(jnp.bfloat16), "row", axis=0, tiled=True)
+    late_gate, late_up, late_down, normed_rows = lax.optimization_barrier(
+        (w_gate, w_up, w_down, normed_rows)
+    )
+    gate_full = jnp.concatenate(gather_parts(late_gate), axis=1)
+    up_full = jnp.concatenate(gather_parts(late_up), axis=1)
+    down_full = gather_natural(late_down, 1)
     qkv_full, out_full = (
         lax.all_gather(joined_projection_weight, "row", axis=0, tiled=True),
         lax.all_gather(output_weight, "row", axis=0, tiled=True),
@@ -139,69 +279,73 @@
             log_totals.append(log_total)
     heads_flat = jnp.concatenate(head_outputs, axis=1)
     row_block = heads_flat
-    attention = lax.psum_scatter(
+    attention = scatter_natural(
         jnp.einsum("tj,dj->td", row_block, out_full, preferred_element_type=jnp.float32),
-        "col",
-        scatter_dimension=0,
-        tiled=True,
+        0,
+        jnp.float32,
     )
     residual = block_input + attention
     mlp_normed, mlp_scale = normalize(residual, mlp_gain)
     mlp_normed = mlp_normed.astype(jnp.bfloat16)
-    slot_of, filled, owner_tok, weight = slot_tables(expert_routes, route_weights)
-    outgoing = jnp.where(filled[:, None], mlp_normed[owner_tok], 0).reshape(E, CAP, -1)
-    gate_full, up_full, down_full = (
-        lax.all_gather(w_gate, "col", axis=1, tiled=True),
-        lax.all_gather(w_up, "col", axis=1, tiled=True),
-        lax.all_gather(w_down, "col", axis=1, tiled=True),
-    )
-    arrived = lax.all_to_all(outgoing, "row", split_axis=0, concat_axis=1, tiled=True)
+    token_rows = lax.all_gather(to_relative(mlp_normed, 1), "row", axis=0, tiled=True)
+
+    def to_slots(rows):
+        return jnp.dot(pick_matrix, rows, preferred_element_type=jnp.float32)
+
+    def to_tokens(rows):
+        partial = lax.dot_general(
+            pick_matrix,
+            rows.reshape(pick_matrix.shape[0], -1),
+            (((0,), (0,)), ((), ())),
+            preferred_element_type=jnp.float32,
+        ).astype(jnp.bfloat16)
+        return lax.psum_scatter(partial, "row", scatter_dimension=0, tiled=True).astype(
+            jnp.float32
+        )
+
+    cot_arrived = (
+        (to_slots(cot_rows_in) * slot_weight.reshape(-1, 1))
+        .astype(jnp.bfloat16)
+        .reshape(experts, -1, cot_rows_in.shape[1])
+    )
+    act_grad = jnp.einsum(
+        "erd,efd->erf", cot_arrived, down_full, preferred_element_type=jnp.float32
+    )
+    arrived = to_slots(token_rows).astype(jnp.bfloat16).reshape(cot_arrived.shape)
     gate_pre = jnp.einsum("erd,edf->erf", arrived, gate_full, preferred_element_type=jnp.float32)
     up_pre = jnp.einsum("erd,edf->erf", arrived, up_full, preferred_element_type=jnp.float32)
     sigmoid_gate = jax.nn.sigmoid(gate_pre)
     active = (gate_pre * sigmoid_gate * up_pre).astype(jnp.bfloat16)
-    produced = jnp.einsum(
-        "erf,efd->erd", active, down_full, preferred_element_type=jnp.float32
-    ).astype(jnp.bfloat16)
-    returned = lax.all_to_all(produced, "row", split_axis=1, concat_axis=0, tiled=True).reshape(
-        E * CAP, -1
-    )
-    picked = returned[slot_of].astype(jnp.float32)
-    block_output = residual + jnp.sum(route_weights[..., None] * picked, axis=1)
-    cot_slots = (
-        jnp.where(filled[:, None], weight[:, None] * out_grad[owner_tok], 0.0)
-        .astype(jnp.bfloat16)
-        .reshape(E, CAP, -1)
-    )
-    cot_arrived = lax.all_to_all(cot_slots, "row", split_axis=0, concat_axis=1, tiled=True)
-    gate_back, up_back, down_back = (gate_full, up_full, down_full)
-    act_grad = jnp.einsum(
-        "erd,efd->erf", cot_arrived, down_back, preferred_element_type=jnp.float32
-    )
-    down_grad = jnp.einsum("erf,erd->efd", active, cot_arrived, preferred_element_type=jnp.float32)
     gate_grad = (act_grad * up_pre * sigmoid_gate * (1.0 + gate_pre * (1.0 - sigmoid_gate))).astype(
         jnp.bfloat16
     )
     up_grad = (act_grad * gate_pre * sigmoid_gate).astype(jnp.bfloat16)
-    gate_w_grad = jnp.einsum("erd,erf->edf", arrived, gate_grad, preferred_element_type=jnp.float32)
-    up_w_grad = jnp.einsum("erd,erf->edf", arrived, up_grad, preferred_element_type=jnp.float32)
-    row_grad = jnp.einsum("erf,edf->erd", gate_grad, gate_back, preferred_element_type=jnp.float32)
+    row_grad = jnp.einsum("erf,edf->erd", gate_grad, gate_full, preferred_element_type=jnp.float32)
     row_grad = (
-        row_grad + jnp.einsum("erf,edf->erd", up_grad, up_back, preferred_element_type=jnp.float32)
-    ).astype(jnp.bfloat16)
-    grad_back = lax.all_to_all(row_grad, "row", split_axis=1, concat_axis=0, tiled=True).reshape(
-        E * CAP, -1
-    )
-    mlp_normed_grad = jnp.sum(grad_back[slot_of].astype(jnp.float32), axis=1)
-    gate_share, up_share, down_share = (
-        lax.psum_scatter(gate_w_grad, "col", scatter_dimension=1, tiled=True),
-        lax.psum_scatter(up_w_grad, "col", scatter_dimension=1, tiled=True),
-        lax.psum_scatter(down_grad, "col", scatter_dimension=1, tiled=True),
-    )
+        row_grad + jnp.einsum("erf,edf->erd", up_grad, up_full, preferred_element_type=jnp.float32)
+    ).astype(jnp.bfloat16)
+    mlp_normed_grad = to_natural(to_tokens(row_grad), 1)
+    gate_w_grad = jnp.einsum(
+        "erd,erf->edf", arrived, gate_grad, preferred_element_type=jnp.float32
+    ).astype(jnp.bfloat16)
+    up_w_grad = jnp.einsum(
+        "erd,erf->edf", arrived, up_grad, preferred_element_type=jnp.float32
+    ).astype(jnp.bfloat16)
+    down_grad = jnp.einsum(
+        "erf,erd->efd", active, cot_arrived, preferred_element_type=jnp.float32
+    ).astype(jnp.bfloat16)
+    gate_share = scatter_relative(gate_w_grad, 1)
+    up_share = scatter_relative(up_w_grad, 1)
+    down_share = scatter_natural(down_grad, 1)
+    produced = (
+        jnp.einsum("erf,efd->erd", active, down_full, preferred_element_type=jnp.float32)
+        * slot_weight[..., None]
+    ).astype(jnp.bfloat16)
+    block_output = residual + to_tokens(produced)
     residual_part, mlp_part = norm_grad(residual, mlp_scale, mlp_gain, mlp_normed_grad)
     residual_grad = out_grad + residual_part
     residual_cotangent = residual_grad.astype(jnp.bfloat16)
-    cot_rows = lax.all_gather(residual_cotangent, "col", axis=0, tiled=True)
+    cot_rows = gather_natural(residual_cotangent, 0)
     heads_cotangent = jnp.einsum(
         "td,dj->tj", cot_rows, out_full, preferred_element_type=jnp.float32
     ).astype(jnp.bfloat16)
@@ -263,19 +407,22 @@
         "td,tj->dj", normed_rows, projected_grad, preferred_element_type=jnp.float32
     )
     qkv_share, out_share = (
-        lax.psum_scatter(qkv_grad_part, "row", scatter_dimension=0, tiled=True),
-        lax.psum_scatter(out_grad_part, "row", scatter_dimension=0, tiled=True),
+        lax.psum_scatter(
+            qkv_grad_part.astype(jnp.bfloat16), "row", scatter_dimension=0, tiled=True
+        ).astype(jnp.float32),
+        lax.psum_scatter(
+            out_grad_part.astype(jnp.bfloat16), "row", scatter_dimension=0, tiled=True
+        ).astype(jnp.float32),
     )
     row_block = projected_grad
-    attn_normed_grad = lax.psum_scatter(
+    attn_normed_grad = scatter_natural(
         jnp.einsum("tj,dj->td", row_block, qkv_full, preferred_element_type=jnp.float32),
-        "col",
-        scatter_dimension=0,
-        tiled=True,
+        0,
+        jnp.float32,
     )
     input_part, attn_part = norm_grad(block_input, attn_scale, attn_gain, attn_normed_grad)
     input_grad = residual_grad + input_part
-    attn_gain_grad, mlp_gain_grad = lax.psum((attn_part, mlp_part), ("row", "col"))
+    attn_gain_grad, mlp_gain_grad = sum_everywhere(jnp.stack([attn_part, mlp_part]))
     return (
         block_output,
         input_grad,

time: 853 us -> 539 us (0.63)
  waiting for transfers between devices: 545 us -> 264 us
  local copies, waits for them, and re-layouts: 66.8 us -> 36 us
  blocking collectives: 73.1 us -> 63.9 us
    reduce_scatter x7 -> x4, waiting for transfers between devices: 321 us -> 137 us  [the longest x2 113 us: to_tokens(): lax.psum_scatter(partial, 'row', scatter_dimension=0, tiled=True)]
    all_to_all x4 -> x0, waiting for transfers between devices: 180 us -> none  [the longest x1 54 us: shards(): lax.all_to_all(outgoing, 'row', split_axis=0, concat_axis=1, tiled=True)]
    ppermute x0 -> x30, waiting for transfers between devices: none -> 120 us  [the longest x10 113 us: col_shift(): return lax.ppermute(values, 'col', pairs)]
    psum x1 -> x0, blocking collectives: 39.5 us -> none  [shards(): lax.psum((attn_part, mlp_part), ('row', 'col'))]
    all_gather x0 -> x1, blocking collectives: none -> 31.1 us  [shards(): lax.all_gather(jnp.concatenate([expert_routes.astype(jnp.float32), route_...]
    gather x6 -> x0, local copies, waits for them, and re-layouts: 30.3 us -> none  [the longest x2 10.3 us: shards(): out_grad[owner_tok]]
    ppermute x0 -> x30, starting transfers between devices: none -> 22.2 us  [the longest x10 12.8 us: col_shift(): return lax.ppermute(values, 'col', pairs)]
    all_gather x1, waiting for transfers between devices: 26.5 us -> 5.86 us  [shards(): lax.all_gather(joined_projection_weight, 'row', axis=0, tiled=True)]
  transfers between devices with their start and end apart: 17 -> 37, of which waited for: 12 -> 13; matrix products, arithmetic and copies ran while one was open for 14% -> 23% of each run, Pallas kernels for 0% -> 0%
where the time goes in v1:
time: 539 us; the launch traced here: 529 us
  waiting for transfers between devices  264 us (49%)
  matrix products  83.5 us (15%)
  blocking collectives  63.9 us (12%)
  other arithmetic  42.1 us (8%)
  local copies, waits for them, and re-layouts  36 us (7%)
  starting transfers between devices  23.1 us (4%)
  between operations  16 us (3%)
    reduce_scatter x2, waiting for transfers between devices, to_tokens(): lax.psum_scatter(partial, 'row', scatter_dimension=0, tiled=True)  113 us
    ppermute x10, waiting for transfers between devices, col_shift(): return lax.ppermute(values, 'col', pairs)  113 us
    all_gather x1, blocking collectives, shards(): lax.all_gather(output_weight, 'row', axis=0, tiled=True)  32.9 us
    all_gather x1, blocking collectives, shards(): lax.all_gather(jnp.concatenate([expert_routes.astype(jnp.float32), route_...  31.1 us
    reduce_scatter x1, waiting for transfers between devices, shards(): lax.psum_scatter(qkv_grad_part.astype(jnp.bfloat16), 'row', scatter_dimen...  24.4 us
    dot_general x2, matrix products, to_tokens(): lax.dot_general(pick_matrix, rows.reshape(pick_matrix.shape[0], -1), (((0...  17.5 us
    unnamed x143, local copies, waits for them, and re-layouts  16.2 us
    ppermute x10, starting transfers between devices, col_shift(): return lax.ppermute(values, 'col', pairs)  12.8 us
  transfers between devices with their start and end apart: 37, of which 13 were waited for; matrix products, arithmetic and copies ran while one was open for 23% of the time, Pallas kernels for 0%

profile of v1, /device:TPU:0, one launch (start us, length us, event | category | flops | bytes accessed | tf_op | source)
XLA Modules:
  0.0 529.1 jit_solution(10819496802319063930)
XLA Ops:
  14.4 32.9 %all_gather.16 = bf16[1024,256]{1,0:T(8,128)(2,1)S(1)} all-gather(bf16[128,256]{1,0:T(8,128)(2,1)S(1)} %copy-done.39), channel_id=1, replica_groups=mesh['row'=8,'col'=4] {'row'}, dimensions={0}, use_global_device_ids=true | all-gather | bytes 589824 | tf_op jit(solution)/shard_map/all_gather | solution.py:249
  49.3 5.9 %all-gather.4.cloned.1.call-done = bf16[1024,512]{1,0:T(8,128)(2,1)} async-done(((bf16[128,512]{1,0:T(8,128)(2,1)}), bf16[1024,512]{1,0:T(8,128)(2,1)}) %all-gather.4.cloned.1.call-update) | async-done | bytes 1048592 | tf_op jit(solution)/shard_map/all_gather | solution.py:248
  57.2 5.2 fusion.26
  74.7 31.1 %all_gather.17 = f32[1024,16]{0,1:T(8,128)S(1)} all-gather(f32[128,16]{0,1:T(8,128)S(1)} %pad_maximum_fusion.5), channel_id=1, replica_groups=mesh['row'=8,'col'=4] {'row'}, dimensions={0}, use_global_device_ids=true | all-gather | bytes 73728 | tf_op jit(solution)/shard_map/all_gather | solution.py:228
  112.0 20.2 %collective-permute-done.11 = bf16[4,128,1024]{2,1,0:T(8,128)(2,1)} collective-permute-done((bf16[4,128,1024]{2,1,0:T(8,128)(2,1)}, bf16[4,128,1024]{2,1,0:T(8,128)(2,1)}, u32[]{:S(2)}, u32[]{:S(2)}) %collective-permute-start.11) | collective-permute-done | bytes 1048608 | tf_op jit(solution)/shard_map/ppermute | solution.py:81
  138.3 16.2 %collective-permute-done.8 = bf16[4,256,512]{2,1,0:T(8,128)(2,1)S(1)} collective-permute-done((bf16[4,256,512]{2,1,0:T(8,128)(2,1)}, bf16[4,256,512]{2,1,0:T(8,128)(2,1)S(1)}, u32[]{:S(2)}, u32[]{:S(2)}) %collective-permute-start.8) | collective-permute-done | bytes 1048608 | tf_op jit(solution)/shard_map/ppermute | solution.py:81
  158.0 11.3 %collective-permute-done.5 = bf16[4,256,512]{2,1,0:T(8,128)(2,1)S(1)} collective-permute-done((bf16[4,256,512]{2,1,0:T(8,128)(2,1)}, bf16[4,256,512]{2,1,0:T(8,128)(2,1)S(1)}, u32[]{:S(2)}, u32[]{:S(2)}) %collective-permute-start.5) | collective-permute-done | bytes 1048608 | tf_op jit(solution)/shard_map/ppermute | solution.py:81
  183.8 4.6 fusion.2
  188.4 5.0 fusion.144
  193.4 4.6 convolution_convert_fusion
  198.0 4.5 fusion.143
  202.5 6.2 %multiply_convert_fusion.3 = (bf16[4,288,512]{2,1,0:T(8,128)(2,1)}, bf16[4,288,512]{2,1,0:T(8,128)(2,1)}, bf16[4,288,512]{2,1,0:T(8,128)(2,1)S(1)}) fusion(f32[4,288,512]{2,1,0:T(8,128)S(1)} %copy-done.8, f32[4,288,512]{2,1,0:T(8,128)S(1)} %fusion.143, bf16[4,288,1024]{2,1,0:T(8,128)(2,1)S(1)} %bitcast.144, ...), kind=kOutput, calls=%fused_computation.16 | convolution fusion | flops 1217396736 | bytes 14811136 | tf_op jit(solution)/shard_map/erd,edf->erf/dot_general | solution.py:315
  208.7 6.2 %fusion.145 = f32[4,288,1024]{2,1,0:T(8,128)} fusion(bf16[4,288,512]{2,1,0:T(8,128)(2,1)S(1)} %get-tuple-element.35, bf16[4,1024,512]{2,1,0:T(8,128)(2,1)} %constant_dynamic-update-slice_fusion.4), kind=kOutput, calls=%fused_computation.281 | convolution fusion | flops 1207959552 | bytes 10092544 | tf_op jit(solution)/shard_map/erf,edf->erd/dot_general | solution.py:325
  214.9 9.4 %bitcast_convert_fusion = bf16[1024,1024]{1,0:T(8,128)(2,1)} fusion(f32[4,288,1024]{2,1,0:T(8,128)} %fusion.145, s32[4,1024]{1,0:T(4,128)S(1)} %fusion.105, bf16[4,288,512]{2,1,0:T(8,128)(2,1)} %get-tuple-element.33, bf16[4,1024,512]{2,1,0:T(8,128)(2,1)} %constant_dynamic-update-slice_fusion), kind=kOutput, calls=%fused_computation.8 | convolution fusion | flops 3628466176 | bytes 12206080 | tf_op jit(solution)/shard_map/dot_general | solution.py:296
  224.4 8.0 %bitcast_convert_fusion.1 = bf16[1024,1024]{1,0:T(8,128)(2,1)} fusion(f32[4,288]{1,0:T(4,128)S(1)} %select_reduce_fusion, s32[4,1024]{1,0:T(4,128)S(1)} %fusion.105, bf16[4,288,512]{2,1,0:T(8,128)(2,1)} %get-tuple-element.34, bf16[4,512,1024]{2,1,0:T(8,128)(2,1)} %constant_dynamic-update-slice_fusion.12), kind=kOutput, calls=%fused_computation.9 | convolution fusion | flops 3628466176 | bytes 7492096 | tf_op jit(solution)/shard_map/dot_general | solution.py:296
  232.8 4.4 convolution_convert_fusion.3
  247.8 43.2 %reduce-scatter.7.cloned.1.call-done = bf16[128,1024]{1,0:T(8,128)(2,1)} async-done(((bf16[1024,1024]{1,0:T(8,128)(2,1)}), bf16[128,1024]{1,0:T(8,128)(2,1)}) %reduce-scatter.7.cloned.1.call-update) | async-done | bytes 262160 | tf_op jit(solution)/shard_map/reduce_scatter | solution.py:302
  292.8 69.7 %reduce-scatter.5.cloned.1.call-done = bf16[128,1024]{1,0:T(8,128)(2,1)} async-done(((bf16[1024,1024]{1,0:T(8,128)(2,1)}), bf16[128,1024]{1,0:T(8,128)(2,1)}) %reduce-scatter.5.cloned.1.call-update) | async-done | bytes 262160 | tf_op jit(solution)/shard_map/reduce_scatter | solution.py:302
  382.5 5.5 %fusion.27 = bf16[512,512]{0,1:T(8,128)(2,1)S(1)} fusion(f32[512,512]{0,1:T(8,128)S(1)} %fusion.32, s32[512]{0:T(512)S(1)} %copy-done.61, s32[512]{0:T(512)S(1)} %copy-done.47, f32[512]{0:T(512)S(1)} %copy-done.63, f32[512]{0:T(512)S(1)} %copy-done.49, s32[512]{0:T(512)S(1)} %copy-done.59, pred[512]{0:T(512)(128)(4,1)S(1)} %copy-done.67, ...), kind=kOutput, calls=%fused_computation.63 | convolution fusion | flops 1614020608 | bytes 1584128 | tf_op jit(solution)/shard_map/dot_general | solution.py:55
  408.0 62.5 %collective-permute-done.18 = bf16[128,1024]{1,0:T(8,128)(2,1)S(1)} collective-permute-done((bf16[128,1024]{1,0:T(8,128)(2,1)}, bf16[128,1024]{1,0:T(8,128)(2,1)S(1)}, u32[]{:S(2)}, u32[]{:S(2)}) %collective-permute-start.18) | collective-permute-done | bytes 262176 | tf_op jit(solution)/shard_map/ppermute | solution.py:81
  471.9 3.6 convert_add_fusion.3
  477.1 3.6 convert_add_fusion.2
  481.5 3.8 fusion.7
  495.7 24.4 %reduce-scatter.9.cloned.1.call-done = bf16[128,512]{1,0:T(8,128)(2,1)} async-done(((bf16[1024,512]{1,0:T(8,128)(2,1)}), bf16[128,512]{1,0:T(8,128)(2,1)}) %reduce-scatter.9.cloned.1.call-update) | async-done | bytes 131088 | tf_op jit(solution)/shard_map/reduce_scatter | solution.py:410
  (329 shorter events, 121.0 us)
Async XLA Ops:
  7.2 47.9 %all-gather.4.cloned.1.call-start = ((), (), s32[]{:S(2)}) async-start(), calls=%async_computation.4 | async-start | bytes 1179648 | tf_op jit(solution)/shard_map/all_gather | solution.py:248
  7.9 175.8 %all-gather.8.cloned.1.call-start = ((), (), s32[]{:S(2)}) async-start(), calls=%async_computation.7 | async-start | bytes 2359296 | tf_op jit(solution)/shard_map/all_gather | solution.py:240
  10.5 37.1 %collective-permute-start = (bf16[128,1024]{1,0:T(8,128)(2,1)S(1)}, bf16[128,1024]{1,0:T(8,128)(2,1)S(1)}, u32[]{:S(2)}, u32[]{:S(2)}) collective-permute-start(bf16[128,1024]{1,0:T(8,128)(2,1)S(1)} %get-tuple-element.32), channel_id=1, source_target_pairs={{0,2},{1,3},{2,0},{3,1},{4,6},{5,7},{6,4},{7,5},{8,10},{9,11},{10,... | collective-permute-start | bytes 786440 | tf_op jit(solution)/shard_map/ppermute | solution.py:81
  13.6 34.3 %collective-permute-start.1 = (bf16[128,1024]{1,0:T(8,128)(2,1)S(1)}, bf16[128,1024]{1,0:T(8,128)(2,1)S(1)}, u32[]{:S(2)}, u32[]{:S(2)}) collective-permute-start(bf16[128,1024]{1,0:T(8,128)(2,1)S(1)} %get-tuple-element.32), channel_id=1, source_target_pairs={{0,1},{1,0},{2,3},{3,2},{4,5},{5,4},{6,7},{7,6},{8,9},{9,8},{10,11... | collective-permute-start | bytes 786440 | tf_op jit(solution)/shard_map/ppermute | solution.py:86
  14.4 179.0 %all-gather.6.cloned.1.call-start = ((), (), s32[]{:S(2)}) async-start(), calls=%async_computation.5 | async-start | bytes 2359296 | tf_op jit(solution)/shard_map/all_gather | solution.py:290
  73.3 33.2 %collective-permute-start.4 = (bf16[128,1024]{1,0:T(8,128)(2,1)S(1)}, bf16[128,1024]{1,0:T(8,128)(2,1)S(1)}, u32[]{:S(2)}, u32[]{:S(2)}) collective-permute-start(bf16[128,1024]{1,0:T(8,128)(2,1)S(1)} %fusion.50), channel_id=1, source_target_pairs={{0,2},{1,3},{2,0},{3,1},{4,6},{5,7},{6,4},{7,5},{8,10},{9,11},{10,... | collective-permute-start | bytes 786440 | tf_op jit(solution)/shard_map/ppermute | solution.py:81
  105.7 26.4 %collective-permute-start.11 = (bf16[4,128,1024]{2,1,0:T(8,128)(2,1)}, bf16[4,128,1024]{2,1,0:T(8,128)(2,1)}, u32[]{:S(2)}, u32[]{:S(2)}) collective-permute-start(bf16[4,128,1024]{2,1,0:T(8,128)(2,1)} %param.22), channel_id=1, source_target_pairs={{0,2},{1,3},{2,0},{3,1},{4,6},{5,7},{6,4},{7,5},{8,10},{9,11},{10,... | collective-permute-start | bytes 3145736 | tf_op jit(solution)/shard_map/ppermute | solution.py:81
  106.5 28.2 %collective-permute-start.12 = (bf16[4,128,1024]{2,1,0:T(8,128)(2,1)}, bf16[4,128,1024]{2,1,0:T(8,128)(2,1)}, u32[]{:S(2)}, u32[]{:S(2)}) collective-permute-start(bf16[4,128,1024]{2,1,0:T(8,128)(2,1)} %param.22), channel_id=1, source_target_pairs={{0,1},{1,0},{2,3},{3,2},{4,5},{5,4},{6,7},{7,6},{8,9},{9,8},{10,11... | collective-permute-start | bytes 3145736 | tf_op jit(solution)/shard_map/ppermute | solution.py:86
  108.7 182.4 %reduce-scatter.7.cloned.1.call-start = ((), (), s32[]{:S(2)}) async-start(), calls=%async_computation.8 | async-start | bytes 2359296 | tf_op jit(solution)/shard_map/reduce_scatter | solution.py:302
  109.5 45.1 %collective-permute-start.8 = (bf16[4,256,512]{2,1,0:T(8,128)(2,1)}, bf16[4,256,512]{2,1,0:T(8,128)(2,1)S(1)}, u32[]{:S(2)}, u32[]{:S(2)}) collective-permute-start(bf16[4,256,512]{2,1,0:T(8,128)(2,1)} %param.21), channel_id=1, source_target_pairs={{0,2},{1,3},{2,0},{3,1},{4,6},{5,7},{6,4},{7,5},{8,10},{9,11},{10,... | collective-permute-start | bytes 3145736 | tf_op jit(solution)/shard_map/ppermute | solution.py:81
  110.8 58.6 %collective-permute-start.5 = (bf16[4,256,512]{2,1,0:T(8,128)(2,1)}, bf16[4,256,512]{2,1,0:T(8,128)(2,1)S(1)}, u32[]{:S(2)}, u32[]{:S(2)}) collective-permute-start(bf16[4,256,512]{2,1,0:T(8,128)(2,1)} %param.20), channel_id=1, source_target_pairs={{0,2},{1,3},{2,0},{3,1},{4,6},{5,7},{6,4},{7,5},{8,10},{9,11},{10,... | collective-permute-start | bytes 3145736 | tf_op jit(solution)/shard_map/ppermute | solution.py:81
  111.9 64.2 %collective-permute-start.9 = (bf16[4,256,512]{2,1,0:T(8,128)(2,1)}, bf16[4,256,512]{2,1,0:T(8,128)(2,1)}, u32[]{:S(2)}, u32[]{:S(2)}) collective-permute-start(bf16[4,256,512]{2,1,0:T(8,128)(2,1)} %param.21), channel_id=1, source_target_pairs={{0,1},{1,0},{2,3},{3,2},{4,5},{5,4},{6,7},{7,6},{8,9},{9,8},{10,11... | collective-permute-start | bytes 3145736 | tf_op jit(solution)/shard_map/ppermute | solution.py:86
  132.2 46.2 %collective-permute-start.6 = (bf16[4,256,512]{2,1,0:T(8,128)(2,1)}, bf16[4,256,512]{2,1,0:T(8,128)(2,1)}, u32[]{:S(2)}, u32[]{:S(2)}) collective-permute-start(bf16[4,256,512]{2,1,0:T(8,128)(2,1)} %param.20), channel_id=1, source_target_pairs={{0,1},{1,0},{2,3},{3,2},{4,5},{5,4},{6,7},{7,6},{8,9},{9,8},{10,11... | collective-permute-start | bytes 3145736 | tf_op jit(solution)/shard_map/ppermute | solution.py:86
  134.7 45.9 %collective-permute-start.13 = (bf16[4,128,1024]{2,1,0:T(8,128)(2,1)}, bf16[4,128,1024]{2,1,0:T(8,128)(2,1)S(1)}, u32[]{:S(2)}, u32[]{:S(2)}) collective-permute-start(bf16[4,128,1024]{2,1,0:T(8,128)(2,1)} %collective-permute-done.11), channel_id=1, source_target_pairs={{0,1},{1,0},{2,3},{3,2},{4,5},{5,4},{6,7},{7,6},{8,9},{9,8},{10,11... | collective-permute-start | bytes 3145736 | tf_op jit(solution)/shard_map/ppermute | solution.py:86
  154.5 27.2 %collective-permute-start.10 = (bf16[4,256,512]{2,1,0:T(8,128)(2,1)S(1)}, bf16[4,256,512]{2,1,0:T(8,128)(2,1)S(1)}, u32[]{:S(2)}, u32[]{:S(2)}) collective-permute-start(bf16[4,256,512]{2,1,0:T(8,128)(2,1)S(1)} %collective-permute-done.8), channel_id=1, source_target_pairs={{0,1},{1,0},{2,3},{3,2},{4,5},{5,4},{6,7},{7,6},{8,9},{9,8},{10,11... | collective-permute-start | bytes 3145736 | tf_op jit(solution)/shard_map/ppermute | solution.py:86
  224.4 138.2 %reduce-scatter.5.cloned.1.call-start = ((), (), s32[]{:S(2)}) async-start(), calls=%async_computation.6 | async-start | bytes 2359296 | tf_op jit(solution)/shard_map/reduce_scatter | solution.py:302
  232.5 252.9 %reduce-scatter.11.cloned.1.call-start = ((), (), s32[]{:S(2)}) async-start(), calls=%async_computation.10 | async-start | bytes 589824 | tf_op jit(solution)/shard_map/reduce_scatter | solution.py:413
  240.3 151.5 %collective-permute-start.24 = (bf16[4,512,512]{2,1,0:T(8,128)(2,1)}, bf16[4,512,512]{2,1,0:T(8,128)(2,1)}, u32[]{:S(2)}, u32[]{:S(2)}) collective-permute-start(bf16[4,512,512]{2,1,0:T(8,128)(2,1)} %slice.119), channel_id=1, source_target_pairs={{0,1},{1,0},{2,3},{3,2},{4,5},{5,4},{6,7},{7,6},{8,9},{9,8},{10,11... | collective-permute-start | bytes 6291464 | tf_op jit(solution)/shard_map/ppermute | solution.py:86
  247.3 148.8 %collective-permute-start.26 = (bf16[4,512,512]{2,1,0:T(8,128)(2,1)}, bf16[4,512,512]{2,1,0:T(8,128)(2,1)}, u32[]{:S(2)}, u32[]{:S(2)}) collective-permute-start(bf16[4,512,512]{2,1,0:T(8,128)(2,1)} %slice.124), channel_id=1, source_target_pairs={{0,1},{1,0},{2,3},{3,2},{4,5},{5,4},{6,7},{7,6},{8,9},{9,8},{10,11... | collective-permute-start | bytes 6291464 | tf_op jit(solution)/shard_map/ppermute | solution.py:86
  391.8 128.4 %reduce-scatter.9.cloned.1.call-start = ((), (), s32[]{:S(2)}) async-start(), calls=%async_computation.9 | async-start | bytes 1179648 | tf_op jit(solution)/shard_map/reduce_scatter | solution.py:410
  394.6 77.3 %collective-permute-start.25 = (bf16[4,256,512]{2,1,0:T(8,128)(2,1)}, bf16[4,256,512]{2,1,0:T(8,128)(2,1)}, u32[]{:S(2)}, u32[]{:S(2)}) collective-permute-start(bf16[4,256,512]{2,1,0:T(8,128)(2,1)} %add_convert_fusion.3), channel_id=1, source_target_pairs={{0,2},{1,3},{2,0},{3,1},{4,6},{5,7},{6,4},{7,5},{8,10},{9,11},{10,... | collective-permute-start | bytes 3145736 | tf_op jit(solution)/shard_map/ppermute | solution.py:81
  398.9 78.2 %collective-permute-start.27 = (bf16[4,256,512]{2,1,0:T(8,128)(2,1)}, bf16[4,256,512]{2,1,0:T(8,128)(2,1)}, u32[]{:S(2)}, u32[]{:S(2)}) collective-permute-start(bf16[4,256,512]{2,1,0:T(8,128)(2,1)} %add_convert_fusion.2), channel_id=1, source_target_pairs={{0,2},{1,3},{2,0},{3,1},{4,6},{5,7},{6,4},{7,5},{8,10},{9,11},{10,... | collective-permute-start | bytes 3145736 | tf_op jit(solution)/shard_map/ppermute | solution.py:81
  402.4 79.1 %collective-permute-start.29 = (bf16[4,128,1024]{2,1,0:T(8,128)(2,1)}, bf16[4,128,1024]{2,1,0:T(8,128)(2,1)}, u32[]{:S(2)}, u32[]{:S(2)}) collective-permute-start(bf16[4,128,1024]{2,1,0:T(8,128)(2,1)} %fusion.6), channel_id=1, source_target_pairs={{0,2},{1,3},{2,0},{3,1},{4,6},{5,7},{6,4},{7,5},{8,10},{9,11},{10,... | collective-permute-start | bytes 3145736 | tf_op jit(solution)/shard_map/ppermute | solution.py:81
  405.7 64.8 %collective-permute-start.18 = (bf16[128,1024]{1,0:T(8,128)(2,1)}, bf16[128,1024]{1,0:T(8,128)(2,1)S(1)}, u32[]{:S(2)}, u32[]{:S(2)}) collective-permute-start(bf16[128,1024]{1,0:T(8,128)(2,1)} %fusion.48), channel_id=1, source_target_pairs={{0,2},{1,3},{2,0},{3,1},{4,6},{5,7},{6,4},{7,5},{8,10},{9,11},{10,... | collective-permute-start | bytes 786440 | tf_op jit(solution)/shard_map/ppermute | solution.py:81
  (82 other events, 539.6 us)
Sparse Core Ops, SparseCore 0:
  10.1 44.9 all-gather.3
  57.8 48.2 all-gather.7
  108.8 47.8 all-gather.5
  224.5 66.5 reduce-scatter.6
  295.0 67.4 reduce-scatter.4
  391.9 61.5 reduce-scatter.10
  456.9 63.2 reduce-scatter.8
